TPU v7x, 32 devices: a whole 2x2x4 slice. The times are simulated.
32 devices in a mesh: groups: 2 (over x), items: 16 (over z, y, core).
Axes of the slice: x: 2, y: 2, z: 4, core: 2. Of those that a mesh axis runs over, the one named last changes fastest.
Arguments:
- candidate_traits: bfloat16 [16384, 2048], P(('groups', 'items')), parts along dimension 0, may hold values from -6 to 6
- candidate_tower_matrix: bfloat16 [2048, 512], replicated, may hold values from -0.125 to 0.125
- query_vectors: bfloat16 [128, 512], P(('groups', 'items')), parts along dimension 0, may hold values from -6 to 6
- kept_positions: int32 [128, 128], P('groups', 'items'), parts along dimension 0, may hold values from 0 to 511
- ranker_first_matrix: bfloat16 [1024, 1024], replicated, may hold values from -0.1875 to 0.1875
- ranker_second_matrix: bfloat16 [1024, 1024], replicated, may hold values from -0.1875 to 0.1875
- ranker_final_vector: bfloat16 [1024], replicated, may hold values from -0.1875 to 0.1875
Outputs:
- prescore: float32 [16384, 64], P(('groups', 'items')), parts along dimension 0
- ranking: float32 [128, 128], P(('groups', 'items')), parts along dimension 0
There are 2 independent parts, one for each index of `groups`. A program takes and returns all parts, laid end to end along the dimension named above; an argument that names none is the same for every part. Nothing has to cross between parts.
Inputs may be any that keep to these rules, and one draw needn't show every extreme that they name: `kept_positions`: entry j of a request is a position within item shard j // 8, which holds items j // 8 * 512 onward.
All inputs are finite; a program needn't handle non-finite values.
Results may differ from a plain program's by a relative error of at most 0.013.
Values may be sent and summed in bfloat16 or wider, within the bound.
A program may use at most 64 MiB of HBM per device.

v0:
```python
import jax
import jax.numpy as jnp
from jax import lax
from jax.sharding import PartitionSpec as P


def item_tower(candidate_traits, candidate_tower_matrix):
    raw = jnp.dot(candidate_traits, candidate_tower_matrix, preferred_element_type=jnp.float32)
    factor = lax.rsqrt(jnp.mean(raw * raw, axis=-1, keepdims=True) + 1e-06)
    return (raw * factor).astype(jnp.bfloat16)


def cross_tower(
    item_rows, user_rows, ranker_first_matrix, ranker_second_matrix, ranker_final_vector
):
    owned, count, width = item_rows.shape
    product = (item_rows.astype(jnp.float32) * user_rows.astype(jnp.float32)[:, None, :]).astype(
        jnp.bfloat16
    )
    cross_in = jnp.concatenate([product, item_rows], axis=-1).reshape(owned * count, 2 * width)
    hidden_one = jax.nn.silu(
        jnp.dot(cross_in, ranker_first_matrix, preferred_element_type=jnp.float32)
    ).astype(jnp.bfloat16)
    hidden_two = jax.nn.silu(
        jnp.dot(hidden_one, ranker_second_matrix, preferred_element_type=jnp.float32)
    ).astype(jnp.bfloat16)
    return jnp.dot(hidden_two, ranker_final_vector, preferred_element_type=jnp.float32).reshape(
        owned, count
    )


def per_device(
    candidate_traits,
    candidate_tower_matrix,
    query_vectors,
    kept_positions,
    ranker_first_matrix,
    ranker_second_matrix,
    ranker_final_vector,
):
    candidate_vectors = item_tower(candidate_traits, candidate_tower_matrix)
    width = candidate_vectors.shape[1]
    all_users = lax.all_gather(query_vectors, "items", axis=0, tiled=True)
    prescore = lax.dot_general(
        candidate_vectors, all_users, (((1,), (1,)), ((), ())), preferred_element_type=jnp.float32
    ) * width ** (-0.5)
    selected_candidates = jnp.take(candidate_vectors, kept_positions, axis=0)
    item_rows = lax.all_to_all(
        selected_candidates, "items", split_axis=0, concat_axis=1, tiled=True
    )
    ranking = cross_tower(
        item_rows, query_vectors, ranker_first_matrix, ranker_second_matrix, ranker_final_vector
    )
    return (prescore, ranking)


def solution(mesh):
    placed = (
        P(("groups", "items"), None),
        P(),
        P(("groups", "items"), None),
        P("groups", "items"),
        P(),
        P(),
        P(),
    )
    return jax.shard_map(
        per_device,
        mesh=mesh,
        in_specs=placed,
        out_specs=(P(("groups", "items"), None), P(("groups", "items"), None)),
        check_vma=False,
    )
```

profile of v0, /device:TPU:0, one launch (start us, length us, event | category | flops | bytes accessed | tf_op | source)
XLA Modules:
  0.0 51.8 jit_solution(16912730754630676367)
XLA Ops:
  0.6 0.0 copy-start
  0.6 0.8 %compare_and_fusion = pred[64,8]{0,1:T(8,128)(4,1)S(1)} fusion(s32[64,8]{0,1:T(8,128)} %param.10), kind=kLoop, calls=%fused_computation.18 | loop fusion | flops 3072 | bytes 2560 | tf_op jit(solution)/shard_map/jit(_take)/and | solution.py:47
  1.5 0.7 %compare_select_fusion = s32[64,8]{0,1:T(8,128)S(1)} fusion(s32[64,8]{0,1:T(8,128)} %param.10), kind=kLoop, calls=%fused_computation.16 | loop fusion | flops 1536 | bytes 4096 | tf_op jit(solution)/shard_map/jit(_take)/jit(_where)/select_n | solution.py:47
  2.2 0.1 copy.18
  2.3 0.1 copy.19
  2.4 0.1 reshape.30
  2.5 3.5 %multiply_reduce_fusion = (f32[512]{0:T(512)S(1)}, f32[512,512]{0,1:T(8,128)S(1)}) fusion(bf16[512,2048]{1,0:T(8,128)(2,1)} %param.7, bf16[2048,512]{1,0:T(8,128)(2,1)} %param.8), kind=kOutput, calls=%fused_computation.14 | convolution fusion | flops 1074265600 | bytes 5244928 | tf_op jit(solution)/shard_map/dot_general | solution.py:8
  6.0 0.1 multiply_convert_fusion.7
  6.1 0.2 copy.20
  6.4 2.6 %gather_fusion = bf16[512,512]{1,0:T(8,128)(2,1)} fusion(bf16[512,512]{1,0:T(8,128)(2,1)S(1)} %copy.20, s32[1024]{0:T(1024)S(1)} %pad_clamp_fusion), kind=kCustom, calls=%fused_computation | custom fusion | bytes 1050624 | tf_op jit(solution)/shard_map/jit(_take)/gather | solution.py:47
  9.0 0.0 copy-start.2
  9.0 0.0 copy-start.1
  9.0 2.0 %bitcast_select_fusion = bf16[64,8,512]{2,1,0:T(8,128)(2,1)} fusion(bf16[512,512]{1,0:T(8,128)(2,1)} %gather_fusion, pred[64,8]{1,0:T(8,128)(4,1)S(1)} %copy.18), kind=kLoop, calls=%fused_computation.15 | loop fusion | flops 262144 | bytes 1049088 | tf_op jit(solution)/shard_map/jit(_take)/select_n | solution.py:47
  11.0 7.4 %all-to-all-start = ((bf16[64,8,512]{2,1,0:T(8,128)(2,1)}), bf16[64,8,512]{2,1,0:T(8,128)(2,1)S(1)}, u32[]{:S(2)}, u32[]{:S(2)}) async-start(bf16[64,8,512]{2,1,0:T(8,128)(2,1)} %bitcast_select_fusion), calls=%async_computation | async-start | bytes 1048576 | tf_op jit(solution)/shard_map/all_to_all | solution.py:48
  18.4 0.0 copy-done.2
  18.4 0.0 copy-done.1
  18.4 25.1 %all-gather = bf16[16,4,512]{2,1,0:T(4,128)(2,1)S(1)} all-gather(bf16[1,4,512]{2,1,0:T(4,128)(2,1)S(1)} %bitcast.24), channel_id=1, replica_groups=mesh['groups'=2,'items'=16] {'items'}, dimensions={0}, use_global_device_ids=true | all-gather | bytes 69632 | tf_op jit(solution)/shard_map/all_gather | solution.py:43
  43.6 0.9 %convolution_multiply_fusion = f32[512,64]{0,1:T(8,128)} fusion(bf16[64,512]{1,0:T(8,128)(2,1)S(1)} %reshape.39, bf16[512,512]{0,1:T(8,128)(2,1)S(1)} %multiply_convert_fusion.7), kind=kOutput, calls=%fused_computation.3 | convolution fusion | flops 33587200 | bytes 720896 | tf_op jit(solution)/shard_map/dot_general | solution.py:44
  44.4 0.0 all-to-all-done
  44.5 0.1 fusion.6
  44.6 0.0 copy-done
  44.6 2.6 %fusion.2 = f32[512,1024]{1,0:T(8,128)} fusion(bf16[1024,1024]{1,0:T(8,128)(2,1)S(1)} %copy-done, bf16[512,512]{1,0:T(8,128)(2,1)S(1)} %bitcast.23, bf16[512,512]{1,0:T(8,128)(2,1)S(1)} %fusion.6), kind=kOutput, calls=%fused_computation.6 | convolution fusion | flops 1075838976 | bytes 5242880 | tf_op jit(solution)/shard_map/dot_general | solution.py:22
  47.2 4.6 %fusion.1 = f32[1,512]{1,0:T(1,128)} fusion(bf16[1024,1]{0,1:T(2,128)(2,1)S(1)} %reshape.40, bf16[1024,1024]{1,0:T(8,128)(2,1)} %param.12, f32[512,1024]{1,0:T(8,128)} %fusion.2), kind=kOutput, calls=%fused_computation.5 | convolution fusion | flops 1080033280 | bytes 4198400 | tf_op jit(solution)/shard_map/dot_general | solution.py:27
  (6 shorter events, 0.1 us)
Async XLA Ops:
  0.6 44.0 %copy-start = (bf16[1024,1024]{1,0:T(8,128)(2,1)S(1)}, bf16[1024,1024]{1,0:T(8,128)(2,1)}, u32[]{:S(2)}) copy-start(bf16[1024,1024]{1,0:T(8,128)(2,1)} %param.11) | copy-start | bytes 6291460
  9.0 9.4 %copy-start.2 = (bf16[1024]{0:T(1024)(128)(2,1)S(1)}, bf16[1024]{0:T(1024)(128)(2,1)}, u32[]{:S(2)}) copy-start(bf16[1024]{0:T(1024)(128)(2,1)} %param.13) | copy-start | bytes 6148
  9.0 9.4 %copy-start.1 = (bf16[4,512]{1,0:T(4,128)(2,1)S(1)}, bf16[4,512]{1,0:T(4,128)(2,1)}, u32[]{:S(2)}) copy-start(bf16[4,512]{1,0:T(4,128)(2,1)} %param.9) | copy-start | bytes 12292
  11.0 33.5 %all-to-all-start = ((bf16[64,8,512]{2,1,0:T(8,128)(2,1)}), bf16[64,8,512]{2,1,0:T(8,128)(2,1)S(1)}, u32[]{:S(2)}, u32[]{:S(2)}) async-start(bf16[64,8,512]{2,1,0:T(8,128)(2,1)} %bitcast_select_fusion), calls=%async_computation | async-start | bytes 1048576 | tf_op jit(solution)/shard_map/all_to_all | solution.py:48
where the time goes:
time: 52.1 us; the launch traced here: 51.8 us
  blocking collectives  25.1 us (48%)
  matrix products  11.6 us (22%)
  starting transfers between devices  7.41 us (14%)
  other arithmetic  3.79 us (7%)
  local copies, waits for them, and re-layouts  3.19 us (6%)
  between operations  0.73 us (1%)
    all_gather x1, blocking collectives, per_device(): all_users = lax.all_gather(query_vectors, 'items', axis=0, tiled=True)  25.1 us
    all_to_all x1, starting transfers between devices, per_device(): lax.all_to_all(selected_candidates, 'items', split_axis=0, concat_axis=1,...  7.41 us
    dot_general x1, matrix products, cross_tower(): jnp.dot(hidden_two, ranker_final_vector, preferred_element_type=jnp.float32)  4.56 us
    dot_general x1, matrix products, item_tower(): jnp.dot(candidate_traits, candidate_tower_matrix, preferred_element_type=...  3.53 us
    select_n x2, other arithmetic, per_device(): selected_candidates = jnp.take(candidate_vectors, kept_positions, axis=0)  2.68 us
    dot_general x1, matrix products, cross_tower(): jnp.dot(cross_in, ranker_first_matrix, preferred_element_type=jnp.float32)  2.63 us
    gather x1, local copies, waits for them, and re-layouts, per_device(): selected_candidates = jnp.take(candidate_vectors, kept_positions, axis=0)  2.61 us
  transfers between devices with their start and end apart: 1, of which 0 were waited for; matrix products, arithmetic and copies ran while one was open for 2% of the time, Pallas kernels for 0%

commit v1 on v0

--- a/solution.py
+++ b/solution.py
@@ -45,8 +45,11 @@
         candidate_vectors, all_users, (((1,), (1,)), ((), ())), preferred_element_type=jnp.float32
     ) * width ** (-0.5)
     selected_candidates = jnp.take(candidate_vectors, kept_positions, axis=0)
-    item_rows = lax.all_to_all(
-        selected_candidates, "items", split_axis=0, concat_axis=1, tiled=True
+    item_rows = jnp.concatenate(
+        lax.all_to_all(
+            jnp.stack(jnp.split(selected_candidates, lax.axis_size("items"), axis=0)), "items", 0, 0
+        ),
+        axis=1,
     )
     ranking = cross_tower(
         item_rows, query_vectors, ranker_first_matrix, ranker_second_matrix, ranker_final_vector

time: 52.1 us -> 61 us (1.17)
  local copies, waits for them, and re-layouts: 3.19 us -> 12.9 us
  other arithmetic: 3.79 us -> 3.01 us
    unnamed x8 -> x23, local copies, waits for them, and re-layouts: 0.04 us -> 9.11 us
    select_n x2, other arithmetic: 2.68 us -> 1.89 us  [per_device(): selected_candidates = jnp.take(candidate_vectors, kept_positions, axis=0)]
  transfers between devices with their start and end apart: 1 -> 1, of which waited for: 0 -> 0; matrix products, arithmetic and copies ran while one was open for 2% -> 1% of each run, Pallas kernels for 0% -> 0%
where the time goes in v1:
time: 61 us; the launch traced here: 60.7 us
  blocking collectives  25.1 us (41%)
  local copies, waits for them, and re-layouts  12.9 us (21%)
  matrix products  11.5 us (19%)
  starting transfers between devices  7.41 us (12%)
  other arithmetic  3.01 us (5%)
  between operations  0.75 us (1%)
    all_gather x1, blocking collectives, per_device(): all_users = lax.all_gather(query_vectors, 'items', axis=0, tiled=True)  25.1 us
    unnamed x23, local copies, waits for them, and re-layouts  9.11 us
    all_to_all x1, starting transfers between devices, per_device(): lax.all_to_all(jnp.stack(jnp.split(selected_candidates, lax.axis_size('it...  7.41 us
    dot_general x1, matrix products, cross_tower(): jnp.dot(hidden_two, ranker_final_vector, preferred_element_type=jnp.float32)  4.54 us
    dot_general x1, matrix products, item_tower(): jnp.dot(candidate_traits, candidate_tower_matrix, preferred_element_type=...  3.53 us
    gather x1, local copies, waits for them, and re-layouts, per_device(): selected_candidates = jnp.take(candidate_vectors, kept_positions, axis=0)  2.61 us
    dot_general x1, matrix products, cross_tower(): jnp.dot(cross_in, ranker_first_matrix, preferred_element_type=jnp.float32)  2.61 us
    select_n x2, other arithmetic, per_device(): selected_candidates = jnp.take(candidate_vectors, kept_positions, axis=0)  1.89 us
  transfers between devices with their start and end apart: 1, of which 0 were waited for; matrix products, arithmetic and copies ran while one was open for 1% of the time, Pallas kernels for 0%

profile of v1, /device:TPU:0, one launch (start us, length us, event | category | flops | bytes accessed | tf_op | source)
XLA Modules:
  0.0 60.7 jit_solution(2488181688227770097)
XLA Ops:
  0.6 0.0 copy-start
  0.6 0.8 %compare_and_fusion = pred[64,8]{0,1:T(8,128)(4,1)S(1)} fusion(s32[64,8]{0,1:T(8,128)} %param.10), kind=kLoop, calls=%fused_computation.50 | loop fusion | flops 3072 | bytes 2560 | tf_op jit(solution)/shard_map/jit(_take)/and | solution.py:47
  1.5 0.7 %compare_select_fusion = s32[64,8]{0,1:T(8,128)S(1)} fusion(s32[64,8]{0,1:T(8,128)} %param.10), kind=kLoop, calls=%fused_computation.48 | loop fusion | flops 1536 | bytes 4096 | tf_op jit(solution)/shard_map/jit(_take)/jit(_where)/select_n | solution.py:47
  2.2 0.1 copy.29
  2.3 0.1 copy.30
  2.4 0.1 reshape.38
  2.5 3.5 %multiply_reduce_fusion = (f32[512]{0:T(512)S(1)}, f32[512,512]{0,1:T(8,128)S(1)}) fusion(bf16[512,2048]{1,0:T(8,128)(2,1)} %param.7, bf16[2048,512]{1,0:T(8,128)(2,1)} %param.8), kind=kOutput, calls=%fused_computation.14 | convolution fusion | flops 1074265600 | bytes 5244928 | tf_op jit(solution)/shard_map/dot_general | solution.py:8
  6.0 0.1 multiply_convert_fusion.7
  6.1 0.2 copy.31
  6.4 2.6 %gather_fusion = bf16[512,512]{1,0:T(8,128)(2,1)} fusion(bf16[512,512]{1,0:T(8,128)(2,1)S(1)} %copy.31, s32[1024]{0:T(1024)S(1)} %pad_clamp_fusion), kind=kCustom, calls=%fused_computation | custom fusion | bytes 1050624 | tf_op jit(solution)/shard_map/jit(_take)/gather | solution.py:47
  9.0 0.0 copy-start.2
  9.0 0.0 copy-start.1
  9.0 1.2 %bitcast_select_fusion = bf16[64,8,512]{2,1,0:T(8,128)(2,1)S(1)} fusion(bf16[512,512]{1,0:T(8,128)(2,1)} %gather_fusion, pred[64,8]{1,0:T(8,128)(4,1)S(1)} %copy.29), kind=kLoop, calls=%fused_computation.15 | loop fusion | flops 262144 | bytes 1049088 | tf_op jit(solution)/shard_map/jit(_take)/select_n | solution.py:47
  10.2 0.6 fusion.24
  10.8 0.6 %fusion.23 = bf16[16,4,8,512]{3,2,1,0:T(8,128)(2,1)} fusion(bf16[16,4,8,512]{3,2,1,0:T(8,128)(2,1)} %fusion.24, bf16[64,8,512]{2,1,0:T(8,128)(2,1)S(1)} %bitcast_select_fusion), kind=kLoop, calls=%fused_computation.45 | loop fusion | bytes 65536
  11.4 0.6 fusion.22
  12.0 0.6 %fusion.21 = bf16[16,4,8,512]{3,2,1,0:T(8,128)(2,1)} fusion(bf16[16,4,8,512]{3,2,1,0:T(8,128)(2,1)} %fusion.22, bf16[64,8,512]{2,1,0:T(8,128)(2,1)S(1)} %bitcast_select_fusion), kind=kLoop, calls=%fused_computation.41 | loop fusion | bytes 65536
  12.6 0.6 fusion.20
  13.2 0.6 %fusion.19 = bf16[16,4,8,512]{3,2,1,0:T(8,128)(2,1)} fusion(bf16[16,4,8,512]{3,2,1,0:T(8,128)(2,1)} %fusion.20, bf16[64,8,512]{2,1,0:T(8,128)(2,1)S(1)} %bitcast_select_fusion), kind=kLoop, calls=%fused_computation.37 | loop fusion | bytes 65536
  13.8 0.6 fusion.18
  14.4 0.6 fusion.17
  15.0 0.6 %fusion.16 = bf16[16,4,8,512]{3,2,1,0:T(8,128)(2,1)} fusion(bf16[16,4,8,512]{3,2,1,0:T(8,128)(2,1)} %fusion.17, bf16[64,8,512]{2,1,0:T(8,128)(2,1)S(1)} %bitcast_select_fusion), kind=kLoop, calls=%fused_computation.31 | loop fusion | bytes 65536
  15.6 0.6 %fusion.15 = bf16[16,4,8,512]{3,2,1,0:T(8,128)(2,1)} fusion(bf16[16,4,8,512]{3,2,1,0:T(8,128)(2,1)} %fusion.16, bf16[64,8,512]{2,1,0:T(8,128)(2,1)S(1)} %bitcast_select_fusion), kind=kLoop, calls=%fused_computation.29 | loop fusion | bytes 65536
  16.3 0.6 fusion.14
  16.9 0.6 fusion.13
  17.5 0.6 fusion.12
  18.1 0.6 fusion.11
  18.7 0.6 fusion.10
  19.3 0.6 %fusion.9 = bf16[16,4,8,512]{3,2,1,0:T(8,128)(2,1)} fusion(bf16[16,4,8,512]{3,2,1,0:T(8,128)(2,1)} %fusion.10, bf16[64,8,512]{2,1,0:T(8,128)(2,1)S(1)} %bitcast_select_fusion), kind=kLoop, calls=%fused_computation.17 | loop fusion | bytes 65536 | tf_op jit(solution)/shard_map/stack | solution.py:50
  19.9 7.4 %all-to-all-start = ((bf16[16,4,8,512]{3,2,1,0:T(8,128)(2,1)}), bf16[16,4,8,512]{3,2,1,0:T(8,128)(2,1)S(1)}, u32[]{:S(2)}, u32[]{:S(2)}) async-start(bf16[16,4,8,512]{3,2,1,0:T(8,128)(2,1)} %fusion.9), calls=%async_computation | async-start | bytes 1048576 | tf_op jit(solution)/shard_map/all_to_all | solution.py:49
  27.3 0.0 copy-done.2
  27.3 0.0 copy-done.1
  27.4 25.1 %all-gather = bf16[16,4,512]{2,1,0:T(4,128)(2,1)S(1)} all-gather(bf16[1,4,512]{2,1,0:T(4,128)(2,1)S(1)} %bitcast.86), channel_id=1, replica_groups=mesh['groups'=2,'items'=16] {'items'}, dimensions={0}, use_global_device_ids=true | all-gather | bytes 69632 | tf_op jit(solution)/shard_map/all_gather | solution.py:43
  52.5 0.9 %convolution_multiply_fusion = f32[512,64]{0,1:T(8,128)} fusion(bf16[64,512]{1,0:T(8,128)(2,1)S(1)} %reshape.47, bf16[512,512]{0,1:T(8,128)(2,1)S(1)} %multiply_convert_fusion.7), kind=kOutput, calls=%fused_computation.3 | convolution fusion | flops 33587200 | bytes 720896 | tf_op jit(solution)/shard_map/dot_general | solution.py:44
  53.3 0.0 all-to-all-done
  53.4 0.1 fusion.6
  53.5 0.0 copy-done
  53.5 2.6 %fusion.2 = f32[512,1024]{1,0:T(8,128)} fusion(bf16[1024,1024]{1,0:T(8,128)(2,1)S(1)} %copy-done, bf16[512,512]{1,0:T(8,128)(2,1)S(1)} %bitcast.85, bf16[512,512]{1,0:T(8,128)(2,1)S(1)} %fusion.6), kind=kOutput, calls=%fused_computation.6 | convolution fusion | flops 1075838976 | bytes 5242880 | tf_op jit(solution)/shard_map/dot_general | solution.py:22
  56.1 4.5 %fusion.1 = f32[1,512]{1,0:T(1,128)} fusion(bf16[1024,1]{0,1:T(2,128)(2,1)S(1)} %reshape.48, bf16[1024,1024]{1,0:T(8,128)(2,1)} %param.12, f32[512,1024]{1,0:T(8,128)} %fusion.2), kind=kOutput, calls=%fused_computation.5 | convolution fusion | flops 1080033280 | bytes 4198400 | tf_op jit(solution)/shard_map/dot_general | solution.py:27
  (6 shorter events, 0.1 us)
Async XLA Ops:
  0.6 52.9 %copy-start = (bf16[1024,1024]{1,0:T(8,128)(2,1)S(1)}, bf16[1024,1024]{1,0:T(8,128)(2,1)}, u32[]{:S(2)}) copy-start(bf16[1024,1024]{1,0:T(8,128)(2,1)} %param.11) | copy-start | bytes 6291460
  9.0 18.3 %copy-start.2 = (bf16[1024]{0:T(1024)(128)(2,1)S(1)}, bf16[1024]{0:T(1024)(128)(2,1)}, u32[]{:S(2)}) copy-start(bf16[1024]{0:T(1024)(128)(2,1)} %param.13) | copy-start | bytes 6148
  9.0 18.3 %copy-start.1 = (bf16[4,512]{1,0:T(4,128)(2,1)S(1)}, bf16[4,512]{1,0:T(4,128)(2,1)}, u32[]{:S(2)}) copy-start(bf16[4,512]{1,0:T(4,128)(2,1)} %param.9) | copy-start | bytes 12292
  19.9 33.5 %all-to-all-start = ((bf16[16,4,8,512]{3,2,1,0:T(8,128)(2,1)}), bf16[16,4,8,512]{3,2,1,0:T(8,128)(2,1)S(1)}, u32[]{:S(2)}, u32[]{:S(2)}) async-start(bf16[16,4,8,512]{3,2,1,0:T(8,128)(2,1)} %fusion.9), calls=%async_computation | async-start | bytes 1048576 | tf_op jit(solution)/shard_map/all_to_all | solution.py:49
